TPU v7x, 32 devices: a whole 2x2x4 slice. The times are simulated.
32 devices in a mesh: wide: 4 (over z), narrow: 8 (over y, x, core).
Axes of the slice: x: 2, y: 2, z: 4, core: 2. Of those that a mesh axis runs over, the one named last changes fastest.
Arguments:
- saved_inputs: bfloat16 [1024, 5120], P('wide', 'narrow'), may hold values from -6 to 6
- out_grads: bfloat16 [1024, 5120], P('wide', 'narrow'), may hold values from -48 to 48
- seq_ids: int32 [1024], P('wide'), may hold values from 0 to 7, as said below
- seq_counts: int32 [8], P('wide'), may hold values from 64 to 192, as said below
- basis_in: bfloat16 [5120, 5120], P('narrow'), may hold values from -0.078125 to 0.078125
- basis_out: bfloat16 [5120, 5120], P('narrow'), may hold values from -0.078125 to 0.078125
- query_rotated: bfloat16 [5120, 5120], P('narrow', 'wide'), may hold values from -6 to 6
- damping: float32 [], replicated, may hold values from 0.05 to 0.5
Outputs:
- eigenvalues: float32 [5120, 5120], P('narrow', 'wide')
- preconditioned: float32 [5120, 5120], P('narrow', 'wide')
Inputs may be any that keep to these rules, and one draw needn't show every extreme that they name: seq_ids names for each token its sequence; the 256 tokens of block w of the token axis belong to the sequences 2 * w to 2 * w + 1, each having at least one token. seq_counts[s] is the number of tokens whose seq_ids equal s.
All inputs are finite; a program needn't handle non-finite values.
Results may differ from a plain program's by a relative error of at most 0.01.
Values may be sent and summed in bfloat16 or wider, within the bound.
No kernel may reach another device: no remote copies, remote signals or barrier semaphores. Data moves between devices by JAX's collectives and lax.ppermute only.
A program may use at most 128 MiB of HBM per device.

v0:
```python
import jax
import jax.numpy as jnp
from jax import lax
from jax.sharding import PartitionSpec as P


def shards(
    saved_inputs, out_grads, seq_ids, seq_counts, basis_in, basis_out, query_rotated, damping
):
    part_in = jnp.dot(saved_inputs, basis_in, preferred_element_type=jnp.float32)
    part_grad = jnp.dot(out_grads, basis_out, preferred_element_type=jnp.float32)
    rot_in = lax.psum(part_in, "narrow").astype(jnp.bfloat16)
    rot_grad = lax.psum_scatter(part_grad, "narrow", scatter_dimension=1, tiled=True).astype(
        jnp.bfloat16
    )
    seq_local = seq_counts.shape[0]
    tok_local = seq_ids.shape[0]
    offset = lax.axis_index("wide") * seq_local
    member = seq_ids[None, :] - offset == jnp.arange(seq_local, dtype=jnp.int32)[:, None]
    weight = (
        jnp.where(member, 1.0, 0.0).astype(jnp.float32) / seq_counts.astype(jnp.float32)[:, None]
    )
    weighted = (rot_grad.astype(jnp.float32)[None, :, :] * weight[:, :, None]).astype(jnp.bfloat16)
    total_seqs = seq_local * lax.axis_size("wide")
    groups = lax.axis_size("wide")
    all_weighted = lax.all_gather(weighted, "wide", axis=0, tiled=True)
    all_weighted = all_weighted.reshape(groups, seq_local, tok_local, all_weighted.shape[2])
    column_rows = lax.all_to_all(rot_in, "wide", split_axis=1, concat_axis=0, tiled=True)
    column_rows = column_rows.reshape(groups, tok_local, column_rows.shape[1])
    per_seq = jnp.einsum(
        "gsti,gtj->gsij", all_weighted, column_rows, preferred_element_type=jnp.float32
    )
    eigenvalues = jnp.sum(per_seq * per_seq, axis=(0, 1)) / total_seqs
    scaled = (query_rotated.astype(jnp.float32) / (eigenvalues + damping)).astype(jnp.bfloat16)
    width = query_rotated.shape[1]
    in_columns = lax.dynamic_slice_in_dim(basis_in, lax.axis_index("wide") * width, width, 1)
    all_scaled, all_columns = (
        lax.all_gather(scaled, "narrow", axis=0, tiled=True),
        lax.all_gather(in_columns, "narrow", axis=0, tiled=True),
    )
    middle = jnp.dot(basis_out, all_scaled, preferred_element_type=jnp.float32).astype(jnp.bfloat16)
    partial_back = lax.dot_general(
        middle, all_columns, (((1,), (1,)), ((), ())), preferred_element_type=jnp.float32
    )
    preconditioned = lax.psum_scatter(partial_back, "wide", scatter_dimension=1, tiled=True)
    return (eigenvalues, preconditioned)


def solution(mesh):
    return jax.shard_map(
        shards,
        mesh=mesh,
        in_specs=(
            P("wide", "narrow"),
            P("wide", "narrow"),
            P("wide"),
            P("wide"),
            P("narrow", None),
            P("narrow", None),
            P("narrow", "wide"),
            P(),
        ),
        out_specs=(P("narrow", "wide"), P("narrow", "wide")),
        check_vma=False,
    )
```

profile of v0, /device:TPU:0, one launch (start us, length us, event | category | flops | bytes accessed | tf_op | source)
XLA Modules:
  0.0 662.8 jit_solution(4311589889708317204)
XLA Ops:
  7.2 0.0 copy-start
  7.2 0.0 reduce-scatter.3.cloned.1.call-start
  7.2 0.9 copy-done
  8.1 7.4 %fusion.3 = f32[256,5120]{1,0:T(8,128)} fusion(bf16[256,640]{1,0:T(8,128)(2,1)S(1)} %copy-done, bf16[640,5120]{1,0:T(8,128)(2,1)} %param.13), kind=kOutput, calls=%fused_computation.13 | convolution fusion | flops 1677721600 | bytes 12124160 | tf_op jit(solution)/shard_map/dot_general | solution.py:11
  15.5 0.0 copy-start.3
  15.5 0.0 reduce-scatter.3.cloned.1.call-update
  15.5 0.9 copy-done.3
  16.5 7.4 %fusion.4 = f32[256,5120]{1,0:T(8,128)} fusion(bf16[256,640]{1,0:T(8,128)(2,1)S(1)} %copy-done.3, bf16[640,5120]{1,0:T(8,128)(2,1)} %param.12), kind=kOutput, calls=%fused_computation.14 | convolution fusion | flops 1677721600 | bytes 12124160 | tf_op jit(solution)/shard_map/dot_general | solution.py:10
  23.9 130.5 %all-reduce.1 = bf16[256,5120]{1,0:T(8,128)(2,1)S(1)} all-reduce(f32[256,5120]{1,0:T(8,128)} %fusion.4), channel_id=1, replica_groups=mesh['wide'=4,'narrow'=8] {'narrow'}, use_global_device_ids=true, to_apply=%region_1.0 | all-reduce | flops 1310720 | bytes 7864320 | tf_op jit(solution)/shard_map/psum | solution.py:12
  154.3 1.7 copy.17
  156.0 0.0 copy-start.5
  156.0 0.0 copy-start.4
  156.0 5.1 all-to-all-start
  161.1 0.0 all-gather.4.cloned.1.call-start
  161.1 0.0 copy-done.5
  161.1 0.0 copy-done.4
  161.1 0.1 fusion.2
  161.2 0.0 reduce-scatter.3.cloned.1.call-done
  161.2 1.1 convert_convert_fusion
  162.3 1.0 multiply_convert_fusion
  163.3 0.0 all-gather.4.cloned.1.call-update
  163.3 0.0 all-gather.6.cloned.1.call-start
  164.0 97.9 %all-to-all-done = bf16[256,4,1280]{2,0,1:T(8,128)(2,1)S(1)} async-done(((bf16[256,4,1280]{2,0,1:T(8,128)(2,1)}), bf16[256,4,1280]{2,0,1:T(8,128)(2,1)S(1)}, u32[]{:S(2)}, u32[]{:S(2)}) %all-to-all-start) | async-done | bytes 2621472 | tf_op jit(solution)/shard_map/all_to_all | solution.py:28
  261.9 0.0 all-gather.4.cloned.1.call-done
  261.9 0.0 copy-start.2
  261.9 6.7 %multiply_reduce_fusion = f32[640,1280]{1,0:T(8,128)S(1)} fusion(bf16[4,2,256,640]{3,2,1,0:T(8,128)(2,1)} %bitcast.30, bf16[256,4,1280]{2,0,1:T(8,128)(2,1)S(1)} %all-to-all-done), kind=kOutput, calls=%fused_computation | convolution fusion | flops 3367731200 | bytes 8519680 | tf_op jit(solution)/shard_map/gsti,gtj->gsij/dot_general | solution.py:30
  268.6 0.0 copy-done.2
  268.6 2.9 divide_convert_fusion
  271.5 0.0 all-gather.6.cloned.1.call-update
  271.5 0.0 all-gather.8.cloned.1.call-start
  271.5 2.7 constant_dynamic-slice_fusion
  274.2 0.0 all-gather.8.cloned.1.call-update
  274.3 0.2 reduce-scatter.5.cloned.1.call-start
  274.5 70.8 %all-gather.6.cloned.1.call-done = bf16[5120,1280]{1,0:T(8,128)(2,1)} async-done(((bf16[640,1280]{1,0:T(8,128)(2,1)}), bf16[5120,1280]{1,0:T(8,128)(2,1)}) %all-gather.6.cloned.1.call-update) | async-done | bytes 13107216 | tf_op jit(solution)/shard_map/all_gather | solution.py:38
  345.3 15.3 %convolution_convert_fusion.clone.4 = bf16[1280,640]{1,0:T(8,128)(2,1)S(1)} fusion(bf16[5120,1280]{1,0:T(8,128)(2,1)} %all-gather.6.cloned.1.call-done, bf16[640,5120]{1,0:T(8,128)(2,1)} %param.13), kind=kOutput, calls=%fused_computation.2.clone.clone.clone.1 | convolution fusion | flops 8389427200 | bytes 21299200 | tf_op jit(solution)/shard_map/dot_general | solution.py:41
  360.6 60.7 %all-gather.8.cloned.1.call-done = bf16[5120,1280]{1,0:T(8,128)(2,1)} async-done(((bf16[640,1280]{1,0:T(8,128)(2,1)}), bf16[5120,1280]{1,0:T(8,128)(2,1)}) %all-gather.8.cloned.1.call-update) | async-done | bytes 13107216 | tf_op jit(solution)/shard_map/all_gather | solution.py:39
  421.2 14.5 %fusion.1 = f32[640,5120]{1,0:T(8,128)} fusion(bf16[5120,1280]{1,0:T(8,128)(2,1)} %all-gather.8.cloned.1.call-done, bf16[1280,640]{1,0:T(8,128)(2,1)S(1)} %convolution_convert_fusion.clone.4), kind=kOutput, calls=%fused_computation.5 | convolution fusion | flops 8388608000 | bytes 27852800 | tf_op jit(solution)/shard_map/dot_general | solution.py:42
  435.8 0.0 reduce-scatter.5.cloned.1.call-update
  435.8 0.0 copy-start.1
  435.8 220.5 %reduce-scatter.5.cloned.1.call-done = f32[640,1280]{1,0:T(8,128)} async-done(((f32[640,5120]{1,0:T(8,128)}), f32[640,1280]{1,0:T(8,128)}) %reduce-scatter.5.cloned.1.call-update) | async-done | bytes 3276816 | tf_op jit(solution)/shard_map/reduce_scatter | solution.py:45
  656.3 0.0 copy-done.1
  (2 shorter events, 0.0 us)
Async XLA Ops:
  7.2 1.0 copy-start
  7.2 154.0 %reduce-scatter.3.cloned.1.call-start = ((), (), s32[]{:S(2)}) async-start(), calls=%async_computation.3 | async-start | bytes 5898240 | tf_op jit(solution)/shard_map/reduce_scatter | solution.py:13
  15.5 1.0 copy-start.3
  156.0 5.1 copy-start.5
  156.0 5.1 copy-start.4
  156.0 105.9 %all-to-all-start = ((bf16[256,4,1280]{2,0,1:T(8,128)(2,1)}), bf16[256,4,1280]{2,0,1:T(8,128)(2,1)S(1)}, u32[]{:S(2)}, u32[]{:S(2)}) async-start(bf16[256,4,1280]{2,0,1:T(8,128)(2,1)} %bitcast.28), calls=%async_computation.1 | async-start | bytes 5242880 | tf_op jit(solution)/shard_map/all_to_all | solution.py:28
  161.1 100.8 %all-gather.4.cloned.1.call-start = ((), (), s32[]{:S(2)}) async-start(), calls=%async_computation.4 | async-start | bytes 3276800 | tf_op jit(solution)/shard_map/all_gather | solution.py:26
  163.3 181.9 %all-gather.6.cloned.1.call-start = ((), (), s32[]{:S(2)}) async-start(), calls=%async_computation.5 | async-start | bytes 14745600 | tf_op jit(solution)/shard_map/all_gather | solution.py:38
  261.9 6.7 %copy-start.2 = (bf16[640,1280]{1,0:T(8,128)(2,1)S(1)}, bf16[640,1280]{1,0:T(8,128)(2,1)}, u32[]{:S(2)}) copy-start(bf16[640,1280]{1,0:T(8,128)(2,1)} %param.14) | copy-start | bytes 4915204
  271.5 149.8 %all-gather.8.cloned.1.call-start = ((), (), s32[]{:S(2)}) async-start(), calls=%async_computation.6 | async-start | bytes 14745600 | tf_op jit(solution)/shard_map/all_gather | solution.py:39
  274.3 382.0 %reduce-scatter.5.cloned.1.call-start = ((), (), s32[]{:S(2)}) async-start(), calls=%async_computation.7 | async-start | bytes 16384000 | tf_op jit(solution)/shard_map/reduce_scatter | solution.py:45
  435.8 220.5 %copy-start.1 = (bf16[256,640]{1,0:T(8,128)(2,1)S(1)}, bf16[256,640]{1,0:T(8,128)(2,1)}, u32[]{:S(2)}) copy-start(bf16[256,640]{1,0:T(8,128)(2,1)} %param.9) | copy-start | bytes 983044
Sparse Core Ops, SparseCore 0:
  15.7 80.4 reduce-scatter.2
  164.0 92.1 all-gather.3
  271.6 73.6 all-gather.5
  347.0 74.1 all-gather.7
  435.9 220.3 reduce-scatter.4
where the time goes:
time: 663 us
  waiting for transfers between devices  450 us (68%)
  blocking collectives  130 us (20%)
  matrix products  51.3 us (8%)
  between operations  14.5 us (2%)
    reduce_scatter x1, waiting for transfers between devices, shards(): lax.psum_scatter(partial_back, 'wide', scatter_dimension=1, tiled=True)  220 us
    psum x1, blocking collectives, shards(): rot_in = lax.psum(part_in, 'narrow').astype(jnp.bfloat16)  130 us
    all_to_all x1, waiting for transfers between devices, shards(): lax.all_to_all(rot_in, 'wide', split_axis=1, concat_axis=0, tiled=True)  97.9 us
    all_gather x1, waiting for transfers between devices, shards(): lax.all_gather(scaled, 'narrow', axis=0, tiled=True)  70.8 us
    all_gather x1, waiting for transfers between devices, shards(): lax.all_gather(in_columns, 'narrow', axis=0, tiled=True)  60.7 us
    dot_general x1, matrix products, shards(): jnp.dot(basis_out, all_scaled, preferred_element_type=jnp.float32)  15.3 us
    dot_general x1, matrix products, shards(): lax.dot_general(middle, all_columns, (((1,), (1,)), ((), ())), preferred_...  14.5 us
  transfers between devices with their start and end apart: 6, of which 4 were waited for; matrix products, arithmetic and copies ran while one was open for 4% of the time, Pallas kernels for 0%

commit v1 on v0

--- a/solution.py
+++ b/solution.py
@@ -9,7 +9,7 @@
 ):
     part_in = jnp.dot(saved_inputs, basis_in, preferred_element_type=jnp.float32)
     part_grad = jnp.dot(out_grads, basis_out, preferred_element_type=jnp.float32)
-    rot_in = lax.psum(part_in, "narrow").astype(jnp.bfloat16)
+    rot_in = jnp.sum(lax.all_gather(part_in, "narrow"), axis=0).astype(jnp.bfloat16)
     rot_grad = lax.psum_scatter(part_grad, "narrow", scatter_dimension=1, tiled=True).astype(
         jnp.bfloat16
     )

time: 663 us -> 787 us (1.19)
  waiting for transfers between devices: 450 us -> 682 us
  blocking collectives: 130 us -> 0 us
  other arithmetic: 5.06 us -> 21.4 us
    all_gather x0 -> x1, waiting for transfers between devices: none -> 197 us  [shards(): lax.all_gather(part_in, 'narrow')]
    psum x1 -> x0, blocking collectives: 130 us -> none  [shards(): rot_in = lax.psum(part_in, 'narrow').astype(jnp.bfloat16)]
    all_to_all x1, waiting for transfers between devices: 97.9 us -> 29.6 us  [shards(): lax.all_to_all(rot_in, 'wide', split_axis=1, concat_axis=0, tiled=True)]
    all_gather x1, waiting for transfers between devices: 0.01 us -> 53.8 us  [shards(): all_weighted = lax.all_gather(weighted, 'wide', axis=0, tiled=True)]
    reduce_scatter x1, waiting for transfers between devices: 0.01 us -> 50.2 us  [shards(): lax.psum_scatter(part_grad, 'narrow', scatter_dimension=1, tiled=True)]
    reduce_sum x0 -> x1, other arithmetic: none -> 16.3 us  [shards(): jnp.sum(lax.all_gather(part_in, 'narrow'), axis=0).astype(jnp.bfloat16)]
  transfers between devices with their start and end apart: 6 -> 7, of which waited for: 4 -> 7; matrix products, arithmetic and copies ran while one was open for 4% -> 6% of each run, Pallas kernels for 0% -> 0%
where the time goes in v1:
time: 787 us; the launch traced here: 786 us
  waiting for transfers between devices  682 us (87%)
  matrix products  51.2 us (7%)
  other arithmetic  21.4 us (3%)
  between operations  14.8 us (2%)
  local copies, waits for them, and re-layouts  12.1 us (2%)
    reduce_scatter x1, waiting for transfers between devices, shards(): lax.psum_scatter(partial_back, 'wide', scatter_dimension=1, tiled=True)  220 us
    all_gather x1, waiting for transfers between devices, shards(): lax.all_gather(part_in, 'narrow')  197 us
    all_gather x1, waiting for transfers between devices, shards(): lax.all_gather(scaled, 'narrow', axis=0, tiled=True)  70 us
    all_gather x1, waiting for transfers between devices, shards(): lax.all_gather(in_columns, 'narrow', axis=0, tiled=True)  60.7 us
    all_gather x1, waiting for transfers between devices, shards(): all_weighted = lax.all_gather(weighted, 'wide', axis=0, tiled=True)  53.8 us
    reduce_scatter x1, waiting for transfers between devices, shards(): lax.psum_scatter(part_grad, 'narrow', scatter_dimension=1, tiled=True)  50.2 us
    all_to_all x1, waiting for transfers between devices, shards(): lax.all_to_all(rot_in, 'wide', split_axis=1, concat_axis=0, tiled=True)  29.6 us
    reduce_sum x1, other arithmetic, shards(): jnp.sum(lax.all_gather(part_in, 'narrow'), axis=0).astype(jnp.bfloat16)  16.3 us
  transfers between devices with their start and end apart: 7, of which 7 were waited for; matrix products, arithmetic and copies ran while one was open for 6% of the time, Pallas kernels for 0%

profile of v1, /device:TPU:0, one launch (start us, length us, event | category | flops | bytes accessed | tf_op | source)
XLA Modules:
  0.0 786.1 jit_solution(5458452755797926333)
XLA Ops:
  7.2 0.0 copy-start
  7.2 0.0 reduce-scatter.3.cloned.1.call-start
  7.2 0.9 copy-done
  8.1 7.3 fusion.3
  15.5 0.0 copy-start.3
  15.5 0.0 reduce-scatter.3.cloned.1.call-update
  15.5 0.0 all-gather.12.cloned.1.call-start
  15.5 0.9 copy-done.3
  16.4 7.4 fusion.4
  23.9 0.0 copy-start.5
  23.9 0.0 copy-start.4
  23.9 0.0 all-gather.12.cloned.1.call-update
  23.9 0.0 all-gather.6.cloned.1.call-start
  24.0 0.6 copy-done.5
  24.5 0.0 copy-done.4
  24.6 0.1 fusion.2
  24.7 50.2 %reduce-scatter.3.cloned.1.call-done = f32[256,640]{1,0:T(8,128)} async-done(((f32[256,5120]{1,0:T(8,128)}), f32[256,640]{1,0:T(8,128)}) %reduce-scatter.3.cloned.1.call-update) | async-done | bytes 655376 | tf_op jit(solution)/shard_map/reduce_scatter | solution.py:13
  74.8 1.1 convert_convert_fusion
  75.9 1.0 multiply_convert_fusion
  76.9 0.0 all-gather.6.cloned.1.call-update
  77.0 196.8 %all-gather.12.cloned.1.call-done = f32[2048,5120]{1,0:T(8,128)} async-done(((f32[256,5120]{1,0:T(8,128)}), f32[2048,5120]{1,0:T(8,128)}) %all-gather.12.cloned.1.call-update) | async-done | bytes 41943056 | tf_op jit(solution)/shard_map/all_gather | solution.py:12
  273.8 16.3 %reduce_sum.18 = bf16[256,5120]{1,0:T(8,128)(2,1)S(1)} reduce(f32[8,256,5120]{2,1,0:T(8,128)} %bitcast.27, f32[]{:T(128)} %constant.5.clone.1), dimensions={0}, to_apply=%region_1.0 | reduce | flops 9175040 | bytes 44564484 | tf_op jit(solution)/shard_map/reduce_sum | solution.py:12
  290.1 2.6 copy.14
  292.6 4.4 copy.15
  297.0 4.6 all-to-all-start
  301.6 0.0 all-gather.8.cloned.1.call-start
  302.3 53.8 %all-gather.6.cloned.1.call-done = bf16[8,256,640]{2,1,0:T(8,128)(2,1)} async-done(((bf16[2,256,640]{2,1,0:T(8,128)(2,1)}), bf16[8,256,640]{2,1,0:T(8,128)(2,1)}) %all-gather.6.cloned.1.call-update) | async-done | bytes 2621456 | tf_op jit(solution)/shard_map/all_gather | solution.py:26
  356.1 29.6 %all-to-all-done = bf16[256,4,1280]{2,0,1:T(8,128)(2,1)S(1)} async-done(((bf16[256,4,1280]{2,0,1:T(8,128)(2,1)}), bf16[256,4,1280]{2,0,1:T(8,128)(2,1)S(1)}, u32[]{:S(2)}, u32[]{:S(2)}) %all-to-all-start) | async-done | bytes 2621472 | tf_op jit(solution)/shard_map/all_to_all | solution.py:28
  385.7 0.0 copy-start.2
  385.7 6.7 multiply_reduce_fusion
  392.4 0.0 copy-done.2
  392.4 2.9 divide_convert_fusion
  395.3 0.0 all-gather.8.cloned.1.call-update
  395.3 0.0 all-gather.10.cloned.1.call-start
  395.4 2.7 constant_dynamic-slice_fusion
  398.1 0.0 all-gather.10.cloned.1.call-update
  398.1 0.2 reduce-scatter.5.cloned.1.call-start
  398.3 70.0 %all-gather.8.cloned.1.call-done = bf16[5120,1280]{1,0:T(8,128)(2,1)} async-done(((bf16[640,1280]{1,0:T(8,128)(2,1)}), bf16[5120,1280]{1,0:T(8,128)(2,1)}) %all-gather.8.cloned.1.call-update) | async-done | bytes 13107216 | tf_op jit(solution)/shard_map/all_gather | solution.py:38
  468.3 15.3 %convolution_convert_fusion.clone.4 = bf16[1280,640]{1,0:T(8,128)(2,1)S(1)} fusion(bf16[5120,1280]{1,0:T(8,128)(2,1)} %all-gather.8.cloned.1.call-done, bf16[640,5120]{1,0:T(8,128)(2,1)} %param.13), kind=kOutput, calls=%fused_computation.2.clone.clone.clone.1 | convolution fusion | flops 8389427200 | bytes 21299200 | tf_op jit(solution)/shard_map/dot_general | solution.py:41
  483.6 60.7 %all-gather.10.cloned.1.call-done = bf16[5120,1280]{1,0:T(8,128)(2,1)} async-done(((bf16[640,1280]{1,0:T(8,128)(2,1)}), bf16[5120,1280]{1,0:T(8,128)(2,1)}) %all-gather.10.cloned.1.call-update) | async-done | bytes 13107216 | tf_op jit(solution)/shard_map/all_gather | solution.py:39
  544.3 14.5 %fusion.1 = f32[640,5120]{1,0:T(8,128)} fusion(bf16[5120,1280]{1,0:T(8,128)(2,1)} %all-gather.10.cloned.1.call-done, bf16[1280,640]{1,0:T(8,128)(2,1)S(1)} %convolution_convert_fusion.clone.4), kind=kOutput, calls=%fused_computation.4 | convolution fusion | flops 8388608000 | bytes 27852800 | tf_op jit(solution)/shard_map/dot_general | solution.py:42
  558.8 0.0 reduce-scatter.5.cloned.1.call-update
  558.8 0.0 copy-start.1
  558.8 220.5 %reduce-scatter.5.cloned.1.call-done = f32[640,1280]{1,0:T(8,128)} async-done(((f32[640,5120]{1,0:T(8,128)}), f32[640,1280]{1,0:T(8,128)}) %reduce-scatter.5.cloned.1.call-update) | async-done | bytes 3276816 | tf_op jit(solution)/shard_map/reduce_scatter | solution.py:45
  779.3 0.0 copy-done.1
  (2 shorter events, 0.0 us)
Async XLA Ops:
  7.2 1.0 copy-start
  7.2 67.6 %reduce-scatter.3.cloned.1.call-start = ((), (), s32[]{:S(2)}) async-start(), calls=%async_computation.3 | async-start | bytes 5898240 | tf_op jit(solution)/shard_map/reduce_scatter | solution.py:13
  15.5 1.0 copy-start.3
  15.5 258.3 %all-gather.12.cloned.1.call-start = ((), (), s32[]{:S(2)}) async-start(), calls=%async_computation.8 | async-start | bytes 47185920 | tf_op jit(solution)/shard_map/all_gather | solution.py:12
  23.9 0.7 copy-start.5
  23.9 0.7 copy-start.4
  23.9 332.2 %all-gather.6.cloned.1.call-start = ((), (), s32[]{:S(2)}) async-start(), calls=%async_computation.4 | async-start | bytes 3276800 | tf_op jit(solution)/shard_map/all_gather | solution.py:26
  297.0 88.7 %all-to-all-start = ((bf16[256,4,1280]{2,0,1:T(8,128)(2,1)}), bf16[256,4,1280]{2,0,1:T(8,128)(2,1)S(1)}, u32[]{:S(2)}, u32[]{:S(2)}) async-start(bf16[256,4,1280]{2,0,1:T(8,128)(2,1)} %copy.15), calls=%async_computation.1 | async-start | bytes 5242880 | tf_op jit(solution)/shard_map/all_to_all | solution.py:28
  301.6 166.7 %all-gather.8.cloned.1.call-start = ((), (), s32[]{:S(2)}) async-start(), calls=%async_computation.5 | async-start | bytes 14745600 | tf_op jit(solution)/shard_map/all_gather | solution.py:38
  385.7 6.7 copy-start.2
  395.3 149.0 %all-gather.10.cloned.1.call-start = ((), (), s32[]{:S(2)}) async-start(), calls=%async_computation.6 | async-start | bytes 14745600 | tf_op jit(solution)/shard_map/all_gather | solution.py:39
  398.1 381.2 %reduce-scatter.5.cloned.1.call-start = ((), (), s32[]{:S(2)}) async-start(), calls=%async_computation.7 | async-start | bytes 16384000 | tf_op jit(solution)/shard_map/reduce_scatter | solution.py:45
  558.8 220.5 %copy-start.1 = (bf16[256,640]{1,0:T(8,128)(2,1)S(1)}, bf16[256,640]{1,0:T(8,128)(2,1)}, u32[]{:S(2)}) copy-start(bf16[256,640]{1,0:T(8,128)(2,1)} %param.9) | copy-start | bytes 983044
Sparse Core Ops, SparseCore 0:
  15.6 59.1 reduce-scatter.2
  76.7 196.9 all-gather.11
  275.3 80.6 all-gather.5
  395.4 72.8 all-gather.7
  470.0 74.1 all-gather.9
  558.9 220.3 reduce-scatter.4
